TPU v7x, 32 devices: a whole 2x2x4 slice. The times are simulated.
32 devices in a mesh: groups: 2 (over x), long: 16 (over z, y, core).
Axes of the slice: x: 2, y: 2, z: 4, core: 2. Of those that a mesh axis runs over, the one named last changes fastest.
Arguments:
- displacement: float32 [4, 2, 128, 16, 256], P('groups', None, 'long'), parts along dimension 0, may hold values from -6 to 6
- velocity: float32 [4, 2, 128, 16, 256], P('groups', None, 'long'), parts along dimension 0, may hold values from -4 to 4
- damage: float32 [4, 128, 16, 256], P('groups', 'long'), parts along dimension 0, may hold values from 0 to 0.6
- material: int32 [4, 128, 16, 256], P('groups', 'long'), parts along dimension 0, may hold values from 0 to 3
- damage_table: float32 [2, 4], replicated, may hold values from 0.1 to 2
- fault_rows: int32 [4, 128, 16], P('groups', 'long'), parts along dimension 0, may hold values from 0 to 3
- kernel: float32 [16, 64, 2, 2], P(None, 'long'), may hold values from -1.5 to 1.5
- history: float32 [30, 64, 2, 2, 16], P('groups', 'long'), parts along dimension 0, may hold values from -6 to 6
Outputs:
- displacement_out: float32 [4, 2, 128, 16, 256], P('groups', None, 'long'), parts along dimension 0
- velocity_out: float32 [4, 2, 128, 16, 256], P('groups', None, 'long'), parts along dimension 0
- damage_out: float32 [4, 128, 16, 256], P('groups', 'long'), parts along dimension 0
- history_out: float32 [30, 64, 2, 2, 16], P('groups', 'long'), parts along dimension 0
There are 2 independent parts, one for each index of `groups`. A program takes and returns all parts, laid end to end along the dimension named above; an argument that names none is the same for every part. Nothing has to cross between parts.
Inputs may be any that keep to these rules, and one draw needn't show every extreme that they name: `fault_rows`: row of the fault face, counted from the fault.
All inputs are finite; a program needn't handle non-finite values.
Results may differ from a plain program's by a relative error of at most 0.00011.
Values sent between devices are 32-bit elements; how exact they have to be, the bound alone decides.
A program may use at most 64 MiB of HBM per device.

v0:
```python
import math
import jax
import jax.numpy as jnp
from jax import lax
from jax.sharding import PartitionSpec as P

STEPS = 2
time_step = 0.5


def padded_2(block, sides, width):
    for axis, dim in sides:
        count = lax.axis_size(axis)
        forward = [(i, i + 1) for i in range(count - 1)]
        forward.append((count - 1, 0))
        backward = [(target, source) for source, target in forward]
        low = lax.ppermute(
            lax.slice_in_dim(block, block.shape[dim] - width, None, axis=dim), axis, forward
        )
        high = lax.ppermute(lax.slice_in_dim(block, 0, width, axis=dim), axis, backward)
        block = jnp.concatenate([low, block, high], axis=dim)
    return block


def class_lookup(material, table_row):
    result = jnp.zeros(material.shape, table_row.dtype)
    for level in range(table_row.shape[0]):
        result = result + jnp.where(
            material == level, table_row[level], jnp.zeros((), table_row.dtype)
        )
    return result


def neighbour(values_in, axis, higher):
    selector = [slice(None)] * values_in.ndim
    for dimension in range(values_in.ndim - 3, values_in.ndim):
        selector[dimension] = slice(1, -1)
    selector[axis] = slice(2, None) if higher else slice(0, -2)
    return values_in[tuple(selector)]


def local_terms(padded_u, padded_c):
    outer_u = jnp.pad(padded_u, ((0, 0), (0, 0), (0, 0), (1, 1), (1, 1)))
    outer_c = jnp.pad(padded_c, ((0, 0), (0, 0), (1, 1), (1, 1)), mode="edge")
    centre_u = outer_u[:, :, 1:-1, 1:-1, 1:-1]
    centre_c = outer_c[:, 1:-1, 1:-1, 1:-1]
    forces = jnp.zeros_like(centre_u)
    energy = jnp.zeros_like(centre_c)
    for offset in range(3):
        above_u = neighbour(outer_u, 2 + offset, True)
        below_u = neighbour(outer_u, 2 + offset, False)
        above_c = neighbour(outer_c, 1 + offset, True)
        below_c = neighbour(outer_c, 1 + offset, False)
        forces = forces + (0.5 * (centre_c + above_c))[None] * (above_u - centre_u)
        forces = forces + (0.5 * (centre_c + below_c))[None] * (below_u - centre_u)
        gradient = 0.5 * (above_u - below_u)
        energy = energy + jnp.sum(gradient * gradient, axis=0)
    return (forces, energy)


def convolve(kernel, stacked):
    kernel_real = kernel[:, :, 0, :, None]
    kernel_imag = kernel[:, :, 1, :, None]
    spec_real = stacked[:, :, 0]
    spec_imag = stacked[:, :, 1]
    out_real = jnp.sum(kernel_real * spec_real - kernel_imag * spec_imag, axis=0)
    out_imag = jnp.sum(kernel_real * spec_imag + kernel_imag * spec_real, axis=0)
    return (out_real, out_imag)


def basis(waves, places, length):
    phase = (waves[:, None] * places[None, :] % length).astype(jnp.float32) * (
        2.0 * math.pi / length
    )
    return (jnp.cos(phase), jnp.sin(phase))


def spectral_terms(cosine, sine_table, slip_part, norming):
    part_real = (
        jnp.einsum("kx,cxz->kcz", cosine, slip_part, precision=lax.Precision.HIGHEST) * norming
    )
    part_imag = (
        -jnp.einsum("kx,cxz->kcz", sine_table, slip_part, precision=lax.Precision.HIGHEST) * norming
    )
    return jnp.stack([part_real, part_imag], 1)


def wave_sum(waves, places, spectrum, length, norming):
    cosine, sine_table = basis(waves, places, length)
    weights = jnp.where(waves == 0, 1.0, 2.0).astype(jnp.float32) * norming
    first_part = jnp.einsum(
        "kx,kcz->cxz", cosine * weights[:, None], spectrum[:, 0], precision=lax.Precision.HIGHEST
    )
    second_part = jnp.einsum(
        "kx,kcz->cxz",
        sine_table * weights[:, None],
        spectrum[:, 1],
        precision=lax.Precision.HIGHEST,
    )
    return first_part - second_part


def advance(
    disp_mid, vel_mid, dmg_mid, rate_mid, limit_mid, fault_mid, forces, energy, traction, signs
):
    pushes = traction[:, None, :, :, None] * signs[None] * fault_mid[None]
    vel_new = vel_mid + time_step * (forces + pushes)
    disp_new = disp_mid + time_step * vel_new
    dmg_new = 1.0 - (1.0 - dmg_mid) * jnp.exp(-rate_mid * jax.nn.softplus(energy - limit_mid))
    return (disp_new, vel_new, dmg_new)


def per_device(displacement, velocity, damage, material, damage_table, fault_rows, kernel, history):
    cells = displacement.shape[2]
    position = lax.axis_index("long")
    length = cells * lax.axis_size("long")
    owned = cells // 2
    norming = 1.0 / math.sqrt(length)
    rates = class_lookup(material, damage_table[0])
    limits = class_lookup(material, damage_table[1])
    heights = lax.broadcasted_iota(jnp.int32, damage.shape, 3)
    on_fault = (heights == fault_rows[..., None]).astype(displacement.dtype)
    signs = jnp.array([1.0, -1.0], displacement.dtype)[:, None, None, None]
    lagged = [history[level] for level in range(history.shape[0])]
    for number in range(STEPS):
        stiffness = 1.0 - damage
        stacked_fields = jnp.concatenate([displacement, stiffness[None]], 0)
        padded = padded_2(stacked_fields, (("long", 2),), 1)
        forces, energy = local_terms(padded[:-1], padded[-1])
        own_disp = displacement
        face = jnp.sum(own_disp * on_fault[None], axis=4)
        slip = face[:, 1] - face[:, 0]
        waves = jnp.arange(lax.axis_size("long") * owned, dtype=jnp.int32)
        places = position * cells + jnp.arange(cells, dtype=jnp.int32)
        cosine, sine_table = basis(waves, places, length)
        current = lax.psum_scatter(
            spectral_terms(cosine, sine_table, slip, norming),
            "long",
            scatter_dimension=0,
            tiled=True,
        )
        stacked_lags = jnp.stack([current] + lagged, 0)
        traction_real, traction_imag = convolve(kernel, stacked_lags)
        traction_spectrum = jnp.stack([traction_real, traction_imag], 1)

        def add_waves(piece):
            waves = jnp.arange(piece.shape[0], dtype=jnp.int32)
            places = position * cells + jnp.arange(cells, dtype=jnp.int32)
            return wave_sum(waves, places, piece, length, norming)

        traction = add_waves(lax.all_gather(traction_spectrum, "long", axis=0, tiled=True))
        displacement, velocity, damage = advance(
            displacement, velocity, damage, rates, limits, on_fault, forces, energy, traction, signs
        )
        lagged = [current] + lagged[:-1]
    return (displacement, velocity, damage, jnp.stack(lagged, 0))


def solution(mesh):
    placed = (
        P("groups", None, "long", None, None),
        P("groups", None, "long", None, None),
        P("groups", "long", None, None),
        P("groups", "long", None, None),
        P(),
        P("groups", "long", None),
        P(None, "long", None, None),
        P("groups", "long", None, None, None),
    )
    return jax.shard_map(
        per_device,
        mesh=mesh,
        in_specs=placed,
        out_specs=(
            P("groups", None, "long", None, None),
            P("groups", None, "long", None, None),
            P("groups", "long", None, None),
            P("groups", "long", None, None, None),
        ),
        check_vma=False,
    )
```

profile of v0, /device:TPU:0, one launch (start us, length us, event | category | flops | bytes accessed | tf_op | source)
XLA Modules:
  0.0 214.8 jit_solution(16481410820871778354)
XLA Ops:
  0.7 1.0 subtract_bitcast_fusion
  1.7 0.9 pad_maximum_fusion.31
  2.6 0.5 collective-permute-start
  3.1 5.1 %collective-permute-start.1 = (f32[3,2,1,16,256]{4,3,2,1,0:T(8,128)S(1)}, f32[3,2,1,16,256]{4,3,2,1,0:T(8,128)S(1)}, u32[]{:S(2)}, u32[]{:S(2)}) collective-permute-start(f32[3,2,1,16,256]{4,3,2,1,0:T(8,128)S(1)} %get-tuple-element.28), channel_id=1, source_target_pairs={{1,0},{2,1},{3,2},{4,3},{5,4},{6,5},{7,6},{8,7},{9,8},{10,9},{11,1... | collective-permute-start | bytes 294920 | tf_op jit(solution)/shard_map/ppermute | solution.py:20
  8.2 0.5 fusion.88
  8.8 0.7 fusion.127
  9.8 0.6 dynamic-slice
  11.0 0.5 select_maximum_fusion.3
  11.5 1.4 multiply_reduce_fusion.5
  12.9 0.2 fusion.7
  13.1 0.3 fusion.8
  13.5 0.7 fusion.38
  14.3 0.9 fusion.122
  15.2 0.1 copy.50
  15.3 62.3 %all-reduce.2 = f32[64,2,2,16]{3,2,1,0:T(2,128)S(1)} all-reduce(f32[64,2,2,16]{3,2,1,0:T(2,128)S(1)} %copy.50), channel_id=2, replica_groups=mesh['groups'=2,'long'=16] {'long'}, use_global_device_ids=true, to_apply=%region_1.2.clone | all-reduce | flops 4096 | bytes 32768
  77.6 0.2 subtract_reduce_fusion.1
  77.9 17.5 %all_gather.6 = f32[64,2,2,16]{3,2,1,0:T(2,128)S(1)} all-gather(f32[4,2,2,16]{3,2,1,0:T(2,128)S(1)} %copy.54), channel_id=1, replica_groups=mesh['groups'=2,'long'=16] {'long'}, dimensions={0}, use_global_device_ids=true | all-gather | bytes 17408 | tf_op jit(solution)/shard_map/all_gather | solution.py:151
  95.6 1.5 fusion.33
  97.1 0.3 fusion.48
  97.4 0.3 fusion.10
  97.8 6.1 %fusion.15 = (f32[2,8,16,256]{3,2,1,0:T(8,128)S(1)}, pred[2,8,16,256]{3,2,1,0:T(8,128)(4,1)}, pred[2,8,16,256]{3,2,1,0:T(8,128)(4,1)}, pred[2,8,16,256]{3,2,1,0:T(8,128)(4,1)}, pred[2,8,16,256]{3,2,1,0:T(8,128)(4,1)}) fusion(f32[2,8,16,256]{3,2,1,0:T(8,128)S(1)} %copy-done.5, f32[2,8,16,256]{3,2,1,0:T(8,128)S(1)} %copy-done.6, ...), kind=kLoop, calls=%fused_computation.57 | loop fusion | flops 2162688 | bytes 1835040 | tf_op jit(solution)/shard_map/sub | solution.py:126
  104.0 1.5 multiply_add_fusion.2
  105.5 0.4 collective-permute-start.2
  105.9 4.1 %collective-permute-start.3 = (f32[3,2,1,16,256]{4,3,2,1,0:T(8,128)S(1)}, f32[3,2,1,16,256]{4,3,2,1,0:T(8,128)S(1)}, u32[]{:S(2)}, u32[]{:S(2)}) collective-permute-start(f32[3,2,1,16,256]{4,3,2,1,0:T(8,128)S(1)} %get-tuple-element.26), channel_id=1, source_target_pairs={{1,0},{2,1},{3,2},{4,3},{5,4},{6,5},{7,6},{8,7},{9,8},{10,9},{11,1... | collective-permute-start | bytes 294920 | tf_op jit(solution)/shard_map/ppermute | solution.py:20
  110.0 0.6 slice.347
  110.7 1.8 collective-permute-done.2
  112.5 0.7 fusion.28
  113.2 0.9 multiply_reduce_fusion.2
  114.1 0.2 fusion.5
  114.4 0.3 fusion.4
  114.6 0.5 select_maximum_fusion
  115.1 1.3 multiply_reduce_fusion.1
  116.5 0.8 fusion.121
  117.2 0.8 copy.57
  118.0 63.8 %all-reduce.3 = f32[64,2,2,16]{3,2,1,0:T(2,128)} all-reduce(f32[64,2,2,16]{3,2,1,0:T(2,128)} %copy.57), channel_id=3, replica_groups=mesh['groups'=2,'long'=16] {'long'}, use_global_device_ids=true, to_apply=%region_8.9.clone | all-reduce | flops 4096 | bytes 32768
  181.8 0.7 dynamic-slice_bitcast_fusion
  182.5 0.2 subtract_reduce_fusion
  182.8 17.5 %all_gather.7 = f32[64,2,2,16]{3,2,1,0:T(2,128)S(1)} all-gather(f32[4,2,2,16]{3,2,1,0:T(2,128)S(1)} %copy.61), channel_id=1, replica_groups=mesh['groups'=2,'long'=16] {'long'}, dimensions={0}, use_global_device_ids=true | all-gather | bytes 17408 | tf_op jit(solution)/shard_map/all_gather | solution.py:151
  200.3 0.7 fusion.125
  200.9 0.9 copy.72
  201.8 0.9 fusion.45
  202.7 0.1 copy.73
  202.9 0.9 fusion.9
  203.8 0.1 broadcast_multiply_fusion
  203.9 1.7 pad_maximum_fusion.27
  205.6 1.3 fusion.23
  207.0 6.2 %fusion.19 = f32[2,8,16,256]{3,2,1,0:T(8,128)} fusion(f32[2,8,16,256]{3,2,1,0:T(8,128)S(1)} %get-tuple-element.18, f32[2,8,16,256]{3,2,1,0:T(8,128)S(1)} %copy-done.9, f32[2,8,16,256]{3,2,1,0:T(8,128)S(1)} %copy-done.10, f32[2,8,16,256]{3,2,1,0:T(8,128)S(1)} %copy-done.8, pred[2,8,16,256]{3,2,1,0:T(8,128)(4,1)S(1)} %copy-done.20, ...), kind=kLoop, calls=%fused_computation.61 | loop fusion | flops 1769472 | bytes 1572896 | tf_op jit(solution)/shard_map/sub | solution.py:109
  213.2 1.6 multiply_add_fusion
  (87 shorter events, 1.1 us)
Async XLA Ops:
  0.6 9.1 %copy-start.27 = (u32[32]{0:T(128)S(1)}, u32[32]{0:T(128)}, u32[]{:S(2)}) copy-start(u32[32]{0:T(128)} %constant.74) | copy-start | bytes 388
  0.6 10.4 %copy-start = (f32[2,2,8,16,256]{4,3,2,1,0:T(8,128)S(1)}, f32[2,2,8,16,256]{4,3,2,1,0:T(8,128)}, u32[]{:S(2)}) copy-start(f32[2,2,8,16,256]{4,3,2,1,0:T(8,128)} %param.9) | copy-start | bytes 1572868
  0.7 8.1 %copy-start.24 = (s32[2,8,16]{2,1,0:T(8,128)S(1)}, s32[2,8,16]{2,1,0:T(8,128)}, u32[]{:S(2)}) copy-start(s32[2,8,16]{2,1,0:T(8,128)} %param.14) | copy-start | bytes 3076
  0.7 8.2 %copy-start.23 = (f32[2,4]{1,0:T(2,128)S(1)}, f32[2,4]{1,0:T(2,128)}, u32[]{:S(2)}) copy-start(f32[2,4]{1,0:T(2,128)} %param.13) | copy-start | bytes 100
  0.7 8.8 %copy-start.25 = (f32[16,4,2,2]{0,3,2,1:T(2,128)S(1)}, f32[16,4,2,2]{0,3,2,1:T(2,128)}, u32[]{:S(2)}) copy-start(f32[16,4,2,2]{0,3,2,1:T(2,128)} %param.15) | copy-start | bytes 3076
  2.6 8.4 %collective-permute-start = (f32[3,2,1,16,256]{4,3,2,1,0:T(8,128)S(1)}, f32[3,2,1,16,256]{4,3,2,1,0:T(8,128)S(1)}, u32[]{:S(2)}, u32[]{:S(2)}) collective-permute-start(f32[3,2,1,16,256]{4,3,2,1,0:T(8,128)S(1)} %get-tuple-element.27), channel_id=1, source_target_pairs={{0,1},{1,2},{2,3},{3,4},{4,5},{5,6},{6,7},{7,8},{8,9},{9,10},{10,1... | collective-permute-start | bytes 294920 | tf_op jit(solution)/shard_map/ppermute | solution.py:17
  3.1 7.9 %collective-permute-start.1 = (f32[3,2,1,16,256]{4,3,2,1,0:T(8,128)S(1)}, f32[3,2,1,16,256]{4,3,2,1,0:T(8,128)S(1)}, u32[]{:S(2)}, u32[]{:S(2)}) collective-permute-start(f32[3,2,1,16,256]{4,3,2,1,0:T(8,128)S(1)} %get-tuple-element.28), channel_id=1, source_target_pairs={{1,0},{2,1},{3,2},{4,3},{5,4},{6,5},{7,6},{8,7},{9,8},{10,9},{11,1... | collective-permute-start | bytes 294920 | tf_op jit(solution)/shard_map/ppermute | solution.py:20
  9.7 67.9 %copy-start.14 = (f32[16,4,2]{2,1,0:T(4,128)}, f32[16,4,2]{2,1,0:T(4,128)S(1)}, u32[]{:S(2)}) copy-start(f32[16,4,2]{2,1,0:T(4,128)S(1)} %copy.53) | copy-start | bytes 1540
  13.5 64.1 %copy-start.11 = (f32[15,4,2,2,16]{4,3,2,1,0:T(2,128)S(1)}, f32[15,4,2,2,16]{4,3,2,1,0:T(2,128)}, u32[]{:S(2)}) copy-start(f32[15,4,2,2,16]{4,3,2,1,0:T(2,128)} %param.16) | copy-start | bytes 46084
  95.4 1.7 copy-start.28
  95.4 2.3 %copy-start.26 = (f32[2]{0:T(128)S(1)}, f32[2]{0:T(128)}, u32[]{:S(2)}) copy-start(f32[2]{0:T(128)} %constant.60.clone) | copy-start | bytes 28
  95.6 2.2 %copy-start.4 = (f32[2,8,16,256]{3,2,1,0:T(8,128)S(1)}, f32[2,8,16,256]{3,2,1,0:T(8,128)}, u32[]{:S(2)}) copy-start(f32[2,8,16,256]{3,2,1,0:T(8,128)} %get-tuple-element.6) | copy-start | bytes 786436
  95.6 2.2 %copy-start.5 = (f32[2,8,16,256]{3,2,1,0:T(8,128)S(1)}, f32[2,8,16,256]{3,2,1,0:T(8,128)}, u32[]{:S(2)}) copy-start(f32[2,8,16,256]{3,2,1,0:T(8,128)} %get-tuple-element.7) | copy-start | bytes 786436
  95.6 2.2 %copy-start.6 = (f32[2,8,16,256]{3,2,1,0:T(8,128)S(1)}, f32[2,8,16,256]{3,2,1,0:T(8,128)}, u32[]{:S(2)}) copy-start(f32[2,8,16,256]{3,2,1,0:T(8,128)} %get-tuple-element.62) | copy-start | bytes 786436
  95.6 2.2 %copy-start.7 = (f32[2,8,16,256]{3,2,1,0:T(8,128)S(1)}, f32[2,8,16,256]{3,2,1,0:T(8,128)}, u32[]{:S(2)}) copy-start(f32[2,8,16,256]{3,2,1,0:T(8,128)} %param.11) | copy-start | bytes 786436
  95.6 2.2 %copy-start.16 = (s32[2,8,16,256]{3,2,1,0:T(8,128)S(1)}, s32[2,8,16,256]{3,2,1,0:T(8,128)}, u32[]{:S(2)}) copy-start(s32[2,8,16,256]{3,2,1,0:T(8,128)} %param.12) | copy-start | bytes 786436
  97.1 6.9 %copy-start.3 = (f32[2,8,16,256]{3,2,1,0:T(8,128)S(1)}, f32[2,8,16,256]{3,2,1,0:T(8,128)}, u32[]{:S(2)}) copy-start(f32[2,8,16,256]{3,2,1,0:T(8,128)} %fusion.38) | copy-start | bytes 786436
  97.1 6.9 %copy-start.13 = (f32[2,2,8,16,256]{4,3,2,1,0:T(8,128)S(1)}, f32[2,2,8,16,256]{4,3,2,1,0:T(8,128)}, u32[]{:S(2)}) copy-start(f32[2,2,8,16,256]{4,3,2,1,0:T(8,128)} %param.10) | copy-start | bytes 1572868
  104.0 6.0 %copy-start.12 = (f32[15,4,2,2,16]{4,3,2,1,0:T(2,128)S(1)}, f32[15,4,2,2,16]{4,3,2,1,0:T(2,128)}, u32[]{:S(2)}) copy-start(f32[15,4,2,2,16]{4,3,2,1,0:T(2,128)} %param.16) | copy-start | bytes 46084
  105.5 6.9 %collective-permute-start.2 = (f32[3,2,1,16,256]{4,3,2,1,0:T(8,128)S(1)}, f32[3,2,1,16,256]{4,3,2,1,0:T(8,128)S(1)}, u32[]{:S(2)}, u32[]{:S(2)}) collective-permute-start(f32[3,2,1,16,256]{4,3,2,1,0:T(8,128)S(1)} %get-tuple-element.25), channel_id=1, source_target_pairs={{0,1},{1,2},{2,3},{3,4},{4,5},{5,6},{6,7},{7,8},{8,9},{9,10},{10,1... | collective-permute-start | bytes 294920 | tf_op jit(solution)/shard_map/ppermute | solution.py:17
  105.9 6.5 %collective-permute-start.3 = (f32[3,2,1,16,256]{4,3,2,1,0:T(8,128)S(1)}, f32[3,2,1,16,256]{4,3,2,1,0:T(8,128)S(1)}, u32[]{:S(2)}, u32[]{:S(2)}) collective-permute-start(f32[3,2,1,16,256]{4,3,2,1,0:T(8,128)S(1)} %get-tuple-element.26), channel_id=1, source_target_pairs={{1,0},{2,1},{3,2},{4,3},{5,4},{6,5},{7,6},{8,7},{9,8},{10,9},{11,1... | collective-permute-start | bytes 294920 | tf_op jit(solution)/shard_map/ppermute | solution.py:20
  112.5 3.9 %copy-start.21 = (f32[2,10,1,256]{3,2,1,0:T(1,128)}, f32[2,10,1,256]{3,2,1,0:T(1,128)S(1)}, u32[]{:S(2)}) copy-start(f32[2,10,1,256]{3,2,1,0:T(1,128)S(1)} %get-tuple-element.43) | copy-start | bytes 61444
  112.5 3.9 %copy-start.22 = (f32[2,10,1,256]{3,2,1,0:T(1,128)}, f32[2,10,1,256]{3,2,1,0:T(1,128)S(1)}, u32[]{:S(2)}) copy-start(f32[2,10,1,256]{3,2,1,0:T(1,128)S(1)} %get-tuple-element.44) | copy-start | bytes 61444
  116.4 66.1 %slice-start = ((f32[15,4,2,2,16]{4,3,2,1,0:T(2,128)}), f32[14,4,2,2,16]{4,3,2,1,0:T(2,128)S(1)}, s32[]{:S(2)}) async-start(f32[15,4,2,2,16]{4,3,2,1,0:T(2,128)} %param.16), calls=%async_computation | async-start | bytes 229376 | tf_op jit(solution)/shard_map/slice | solution.py:124
  116.4 66.2 %copy-start.15 = (f32[16,4,2]{2,1,0:T(4,128)S(1)}, f32[16,4,2]{2,1,0:T(4,128)}, u32[]{:S(2)}) copy-start(f32[16,4,2]{2,1,0:T(4,128)} %copy-done.14) | copy-start | bytes 1540
  203.9 3.1 %copy-start.8 = (f32[2,8,16,256]{3,2,1,0:T(8,128)S(1)}, f32[2,8,16,256]{3,2,1,0:T(8,128)}, u32[]{:S(2)}) copy-start(f32[2,8,16,256]{3,2,1,0:T(8,128)} %get-tuple-element.4) | copy-start | bytes 786436
  203.9 3.1 %copy-start.9 = (f32[2,8,16,256]{3,2,1,0:T(8,128)S(1)}, f32[2,8,16,256]{3,2,1,0:T(8,128)}, u32[]{:S(2)}) copy-start(f32[2,8,16,256]{3,2,1,0:T(8,128)} %get-tuple-element.5) | copy-start | bytes 786436
  203.9 3.1 %copy-start.10 = (f32[2,8,16,256]{3,2,1,0:T(8,128)S(1)}, f32[2,8,16,256]{3,2,1,0:T(8,128)}, u32[]{:S(2)}) copy-start(f32[2,8,16,256]{3,2,1,0:T(8,128)} %get-tuple-element.8) | copy-start | bytes 786436
  203.9 3.1 %copy-start.17 = (pred[2,8,16,256]{3,2,1,0:T(8,128)(4,1)S(1)}, pred[2,8,16,256]{3,2,1,0:T(8,128)(4,1)}, u32[]{:S(2)}) copy-start(pred[2,8,16,256]{3,2,1,0:T(8,128)(4,1)} %get-tuple-element.19) | copy-start | bytes 196612
  203.9 3.1 %copy-start.18 = (pred[2,8,16,256]{3,2,1,0:T(8,128)(4,1)S(1)}, pred[2,8,16,256]{3,2,1,0:T(8,128)(4,1)}, u32[]{:S(2)}) copy-start(pred[2,8,16,256]{3,2,1,0:T(8,128)(4,1)} %get-tuple-element.20) | copy-start | bytes 196612
  203.9 3.1 %copy-start.19 = (pred[2,8,16,256]{3,2,1,0:T(8,128)(4,1)S(1)}, pred[2,8,16,256]{3,2,1,0:T(8,128)(4,1)}, u32[]{:S(2)}) copy-start(pred[2,8,16,256]{3,2,1,0:T(8,128)(4,1)} %get-tuple-element.21) | copy-start | bytes 196612
  203.9 3.1 %copy-start.20 = (pred[2,8,16,256]{3,2,1,0:T(8,128)(4,1)S(1)}, pred[2,8,16,256]{3,2,1,0:T(8,128)(4,1)}, u32[]{:S(2)}) copy-start(pred[2,8,16,256]{3,2,1,0:T(8,128)(4,1)} %get-tuple-element.22) | copy-start | bytes 196612
  206.9 6.3 %copy-start.1 = (f32[2,2,8,16,256]{4,3,2,1,0:T(8,128)S(1)}, f32[2,2,8,16,256]{4,3,2,1,0:T(8,128)}, u32[]{:S(2)}) copy-start(f32[2,2,8,16,256]{4,3,2,1,0:T(8,128)} %get-tuple-element.24) | copy-start | bytes 1572868
  207.0 6.3 %copy-start.2 = (f32[2,8,16,256]{3,2,1,0:T(8,128)S(1)}, f32[2,8,16,256]{3,2,1,0:T(8,128)}, u32[]{:S(2)}) copy-start(f32[2,8,16,256]{3,2,1,0:T(8,128)} %fusion.28) | copy-start | bytes 786436
where the time goes:
time: 215 us
  blocking collectives  161 us (75%)
  other arithmetic  29.3 us (14%)
  starting transfers between devices  10.1 us (5%)
  local copies, waits for them, and re-layouts  7.45 us (3%)
  matrix products  3.4 us (2%)
    unnamed x2, blocking collectives  126 us
    all_gather x2, blocking collectives, per_device(): lax.all_gather(traction_spectrum, 'long', axis=0, tiled=True)  35 us
    ppermute x2, starting transfers between devices, padded_2(): lax.ppermute(lax.slice_in_dim(block, 0, width, axis=dim), axis, backward)  9.16 us
    sub x1, other arithmetic, advance(): 1.0 - (1.0 - dmg_mid) * jnp.exp(-rate_mid * jax.nn.softplus(energy - limi...  6.16 us
    sub x1, other arithmetic, per_device(): stiffness = 1.0 - damage  6.15 us
  transfers between devices with their start and end apart: 4, of which 1 were waited for; matrix products, arithmetic and copies ran while one was open for 1% of the time, Pallas kernels for 0%

commit v1 on v0

--- a/solution.py
+++ b/solution.py
@@ -6,6 +6,18 @@
 
 STEPS = 2
 time_step = 0.5
+
+
+def place_the_blocks(sheet):
+    formed, fresh = (lax.axis_size("long"), lax.axis_index("long"))
+    left_arr, top = (sheet, 1)
+    while top < formed:
+        u1 = lax.ppermute(left_arr, "long", [(ii, ii ^ top) for ii in range(formed)])
+        y1 = jnp.concatenate([left_arr, u1], axis=0)
+        z_new = jnp.concatenate([u1, left_arr], axis=0)
+        left_arr = jnp.where(fresh & top == 0, y1, z_new)
+        top = 2 * top
+    return left_arr
 
 
 def padded_2(block, sides, width):
@@ -148,7 +160,7 @@
             places = position * cells + jnp.arange(cells, dtype=jnp.int32)
             return wave_sum(waves, places, piece, length, norming)
 
-        traction = add_waves(lax.all_gather(traction_spectrum, "long", axis=0, tiled=True))
+        traction = add_waves(place_the_blocks(traction_spectrum))
         displacement, velocity, damage = advance(
             displacement, velocity, damage, rates, limits, on_fault, forces, energy, traction, signs
         )

time: 215 us -> 191 us (0.89)
  blocking collectives: 161 us -> 125 us
  waiting for transfers between devices: 1.76 us -> 22.3 us
  local copies, waits for them, and re-layouts: 7.45 us -> 2.75 us
  other arithmetic: 29.3 us -> 25.7 us
    all_gather x2 -> x0, blocking collectives: 35 us -> none  [per_device(): lax.all_gather(traction_spectrum, 'long', axis=0, tiled=True)]
    ppermute x0 -> x8, waiting for transfers between devices: none -> 20 us  [place_the_blocks(): lax.ppermute(left_arr, 'long', [(ii, ii ^ top) for ii in range(formed)])]
  transfers between devices with their start and end apart: 4 -> 12, of which waited for: 1 -> 6; matrix products, arithmetic and copies ran while one was open for 1% -> 10% of each run, Pallas kernels for 0% -> 0%
where the time goes in v1:
time: 191 us; the launch traced here: 190 us
  blocking collectives  125 us (65%)
  other arithmetic  25.7 us (13%)
  waiting for transfers between devices  22.3 us (12%)
  starting transfers between devices  10.6 us (6%)
  local copies, waits for them, and re-layouts  2.75 us (1%)
  matrix products  2.18 us (1%)
  between operations  1.96 us (1%)
    unnamed x2, blocking collectives  125 us
    ppermute x8, waiting for transfers between devices, place_the_blocks(): lax.ppermute(left_arr, 'long', [(ii, ii ^ top) for ii in range(formed)])  20 us
    ppermute x2, starting transfers between devices, padded_2(): lax.ppermute(lax.slice_in_dim(block, 0, width, axis=dim), axis, backward)  9.49 us
    sub x1, other arithmetic, per_device(): stiffness = 1.0 - damage  7.59 us
    sub x1, other arithmetic, advance(): 1.0 - (1.0 - dmg_mid) * jnp.exp(-rate_mid * jax.nn.softplus(energy - limi...  6.35 us
  transfers between devices with their start and end apart: 12, of which 6 were waited for; matrix products, arithmetic and copies ran while one was open for 10% of the time, Pallas kernels for 0%

profile of v1, /device:TPU:0, one launch (start us, length us, event | category | flops | bytes accessed | tf_op | source)
XLA Modules:
  0.0 190.5 jit_solution(17013212001108436277)
XLA Ops:
  0.7 1.0 subtract_bitcast_fusion
  1.7 0.9 pad_maximum_fusion.31
  2.6 0.5 collective-permute-start
  3.1 5.1 %collective-permute-start.1 = (f32[3,2,1,16,256]{4,3,2,1,0:T(8,128)S(1)}, f32[3,2,1,16,256]{4,3,2,1,0:T(8,128)S(1)}, u32[]{:S(2)}, u32[]{:S(2)}) collective-permute-start(f32[3,2,1,16,256]{4,3,2,1,0:T(8,128)S(1)} %get-tuple-element.28), channel_id=1, source_target_pairs={{1,0},{2,1},{3,2},{4,3},{5,4},{6,5},{7,6},{8,7},{9,8},{10,9},{11,1... | collective-permute-start | bytes 294920 | tf_op jit(solution)/shard_map/ppermute | solution.py:32
  8.2 0.6 fusion.84
  8.8 0.1 fusion.40
  8.9 0.7 fusion.121
  9.6 0.1 copy.49
  9.7 0.1 copy.53
  9.8 0.6 dynamic-slice
  11.1 0.5 select_maximum_fusion.3
  11.6 1.4 multiply_reduce_fusion.5
  12.9 0.2 fusion.7
  13.2 0.3 fusion.8
  13.6 0.1 copy.50
  13.7 62.1 %all-reduce.2 = f32[64,2,2,16]{3,2,1,0:T(2,128)S(1)} all-reduce(f32[64,2,2,16]{3,2,1,0:T(2,128)S(1)} %copy.50), channel_id=2, replica_groups=mesh['groups'=2,'long'=16] {'long'}, use_global_device_ids=true, to_apply=%region_1.2.clone | all-reduce | flops 4096 | bytes 32768
  75.9 0.2 subtract_reduce_fusion.1
  76.1 0.1 copy.54
  76.4 7.6 %fusion.15 = (f32[2,8,16,256]{3,2,1,0:T(8,128)S(1)}, pred[2,8,16,256]{3,2,1,0:T(8,128)(4,1)}, pred[2,8,16,256]{3,2,1,0:T(8,128)(4,1)}, pred[2,8,16,256]{3,2,1,0:T(8,128)(4,1)}, pred[2,8,16,256]{3,2,1,0:T(8,128)(4,1)}) fusion(f32[2,8,16,256]{3,2,1,0:T(8,128)} %get-tuple-element.7, f32[2,8,16,256]{3,2,1,0:T(8,128)} %get-tuple-element.58, ...), kind=kLoop, calls=%fused_computation.57 | loop fusion | flops 2162688 | bytes 1835040 | tf_op jit(solution)/shard_map/sub | solution.py:138
  84.2 0.1 fusion.118
  84.3 3.8 %collective-permute-done.3 = f32[8,2,2,16]{0,3,2,1:T(8,128)S(1)} collective-permute-done((f32[8,2,2,16]{0,3,2,1:T(8,128)S(1)}, f32[8,2,2,16]{0,3,2,1:T(8,128)S(1)}, u32[]{:S(2)}, u32[]{:S(2)}) %collective-permute-start.3) | collective-permute-done | bytes 2080 | tf_op jit(solution)/shard_map/ppermute | solution.py:15
  88.3 0.3 fusion.33
  88.7 3.5 %collective-permute-done.4 = f32[16,2,2,16]{0,3,2,1:T(8,128)S(1)} collective-permute-done((f32[16,2,2,16]{0,3,2,1:T(8,128)S(1)}, f32[16,2,2,16]{0,3,2,1:T(8,128)S(1)}, u32[]{:S(2)}, u32[]{:S(2)}) %collective-permute-start.4) | collective-permute-done | bytes 4128 | tf_op jit(solution)/shard_map/ppermute | solution.py:15
  92.4 4.8 %collective-permute-done.5 = f32[32,2,2,16]{0,3,2,1:T(8,128)S(1)} collective-permute-done((f32[32,2,2,16]{0,3,2,1:T(8,128)S(1)}, f32[32,2,2,16]{0,3,2,1:T(8,128)S(1)}, u32[]{:S(2)}, u32[]{:S(2)}) %collective-permute-start.5) | collective-permute-done | bytes 8224 | tf_op jit(solution)/shard_map/ppermute | solution.py:15
  97.3 0.3 fusion.45
  97.5 0.3 fusion.10
  98.0 1.5 multiply_add_fusion.2
  99.6 4.4 %collective-permute-start.7 = (f32[3,2,1,16,256]{4,3,2,1,0:T(8,128)S(1)}, f32[3,2,1,16,256]{4,3,2,1,0:T(8,128)S(1)}, u32[]{:S(2)}, u32[]{:S(2)}) collective-permute-start(f32[3,2,1,16,256]{4,3,2,1,0:T(8,128)S(1)} %get-tuple-element.26), channel_id=1, source_target_pairs={{1,0},{2,1},{3,2},{4,3},{5,4},{6,5},{7,6},{8,7},{9,8},{10,9},{11,1... | collective-permute-start | bytes 294920 | tf_op jit(solution)/shard_map/ppermute | solution.py:32
  104.0 2.3 %collective-permute-done.6 = f32[3,2,1,16,256]{4,3,2,1,0:T(8,128)S(1)} collective-permute-done((f32[3,2,1,16,256]{4,3,2,1,0:T(8,128)S(1)}, f32[3,2,1,16,256]{4,3,2,1,0:T(8,128)S(1)}, u32[]{:S(2)}, u32[]{:S(2)}) %collective-permute-start.6) | collective-permute-done | bytes 98336 | tf_op jit(solution)/shard_map/ppermute | solution.py:29
  106.3 0.2 multiply_reduce_fusion.2
  106.5 0.3 fusion.5
  106.7 0.3 fusion.4
  107.2 0.1 fusion.117
  107.3 0.1 copy.56
  107.4 62.8 %all-reduce.3 = f32[64,2,2,16]{3,2,1,0:T(2,128)S(1)} all-reduce(f32[64,2,2,16]{3,2,1,0:T(2,128)S(1)} %copy.56), channel_id=3, replica_groups=mesh['groups'=2,'long'=16] {'long'}, use_global_device_ids=true, to_apply=%region_8.9.clone | all-reduce | flops 4096 | bytes 32768
  170.4 0.2 subtract_reduce_fusion
  170.6 0.1 copy.60
  170.9 0.3 fusion.23
  171.2 0.5 select_maximum_fusion
  171.7 0.5 multiply_reduce_fusion.1
  172.4 0.1 copy-done.6
  172.6 6.4 %fusion.19 = f32[2,8,16,256]{3,2,1,0:T(8,128)} fusion(f32[2,8,16,256]{3,2,1,0:T(8,128)S(1)} %get-tuple-element.18, f32[2,8,16,256]{3,2,1,0:T(8,128)S(1)} %get-tuple-element.5, f32[2,8,16,256]{3,2,1,0:T(8,128)S(1)} %get-tuple-element.8, f32[2,8,16,256]{3,2,1,0:T(8,128)S(1)} %get-tuple-element.4, pred[2,8,16,256]{3,2,1,0:T(8,128)(4,1)S(1)} %copy-done.9, ...), kind=kLoop, calls=%fused_computation.61 | loop fusion | flops 1769472 | bytes 1572896 | tf_op jit(solution)/shard_map/sub | solution.py:121
  179.2 3.9 %collective-permute-done.10 = f32[16,2,2,16]{0,3,2,1:T(8,128)S(1)} collective-permute-done((f32[16,2,2,16]{0,3,2,1:T(8,128)S(1)}, f32[16,2,2,16]{0,3,2,1:T(8,128)S(1)}, u32[]{:S(2)}, u32[]{:S(2)}) %collective-permute-start.10) | collective-permute-done | bytes 4128 | tf_op jit(solution)/shard_map/ppermute | solution.py:15
  183.2 0.7 pad_maximum_fusion.27
  183.9 4.1 %collective-permute-done.11 = f32[32,2,2,16]{0,3,2,1:T(8,128)S(1)} collective-permute-done((f32[32,2,2,16]{0,3,2,1:T(8,128)S(1)}, f32[32,2,2,16]{0,3,2,1:T(8,128)S(1)}, u32[]{:S(2)}, u32[]{:S(2)}) %collective-permute-start.11) | collective-permute-done | bytes 8224 | tf_op jit(solution)/shard_map/ppermute | solution.py:15
  188.1 0.3 fusion.44
  188.4 0.3 fusion.9
  188.8 1.7 multiply_add_fusion
  (82 shorter events, 2.3 us)
Async XLA Ops:
  0.6 9.2 %copy-start.14 = (u32[32]{0:T(128)S(1)}, u32[32]{0:T(128)}, u32[]{:S(2)}) copy-start(u32[32]{0:T(128)} %constant.78) | copy-start | bytes 388
  0.6 10.4 %copy-start = (f32[2,2,8,16,256]{4,3,2,1,0:T(8,128)S(1)}, f32[2,2,8,16,256]{4,3,2,1,0:T(8,128)}, u32[]{:S(2)}) copy-start(f32[2,2,8,16,256]{4,3,2,1,0:T(8,128)} %param.9) | copy-start | bytes 1572868
  0.7 8.1 %copy-start.11 = (s32[2,8,16]{2,1,0:T(8,128)S(1)}, s32[2,8,16]{2,1,0:T(8,128)}, u32[]{:S(2)}) copy-start(s32[2,8,16]{2,1,0:T(8,128)} %param.14) | copy-start | bytes 3076
  0.7 8.2 %copy-start.10 = (f32[2,4]{1,0:T(2,128)S(1)}, f32[2,4]{1,0:T(2,128)}, u32[]{:S(2)}) copy-start(f32[2,4]{1,0:T(2,128)} %param.13) | copy-start | bytes 100
  0.7 8.9 %copy-start.12 = (f32[16,4,2,2]{0,3,2,1:T(2,128)S(1)}, f32[16,4,2,2]{0,3,2,1:T(2,128)}, u32[]{:S(2)}) copy-start(f32[16,4,2,2]{0,3,2,1:T(2,128)} %param.15) | copy-start | bytes 3076
  2.6 8.5 %collective-permute-start = (f32[3,2,1,16,256]{4,3,2,1,0:T(8,128)S(1)}, f32[3,2,1,16,256]{4,3,2,1,0:T(8,128)S(1)}, u32[]{:S(2)}, u32[]{:S(2)}) collective-permute-start(f32[3,2,1,16,256]{4,3,2,1,0:T(8,128)S(1)} %get-tuple-element.27), channel_id=1, source_target_pairs={{0,1},{1,2},{2,3},{3,4},{4,5},{5,6},{6,7},{7,8},{8,9},{9,10},{10,1... | collective-permute-start | bytes 294920 | tf_op jit(solution)/shard_map/ppermute | solution.py:29
  3.1 8.0 %collective-permute-start.1 = (f32[3,2,1,16,256]{4,3,2,1,0:T(8,128)S(1)}, f32[3,2,1,16,256]{4,3,2,1,0:T(8,128)S(1)}, u32[]{:S(2)}, u32[]{:S(2)}) collective-permute-start(f32[3,2,1,16,256]{4,3,2,1,0:T(8,128)S(1)} %get-tuple-element.28), channel_id=1, source_target_pairs={{1,0},{2,1},{3,2},{4,3},{5,4},{6,5},{7,6},{8,7},{9,8},{10,9},{11,1... | collective-permute-start | bytes 294920 | tf_op jit(solution)/shard_map/ppermute | solution.py:32
  9.8 66.1 %copy-start.4 = (f32[16,4,2]{2,1,0:T(4,128)}, f32[16,4,2]{2,1,0:T(4,128)S(1)}, u32[]{:S(2)}) copy-start(f32[16,4,2]{2,1,0:T(4,128)S(1)} %copy.53) | copy-start | bytes 1540
  12.9 62.9 %copy-start.2 = (f32[15,4,2,2,16]{4,3,2,1,0:T(2,128)S(1)}, f32[15,4,2,2,16]{4,3,2,1,0:T(2,128)}, u32[]{:S(2)}) copy-start(f32[15,4,2,2,16]{4,3,2,1,0:T(2,128)} %param.16) | copy-start | bytes 46084
  76.3 7.8 %collective-permute-start.2 = (f32[4,2,2,16]{0,3,2,1:T(8,128)S(1)}, f32[4,2,2,16]{0,3,2,1:T(8,128)S(1)}, u32[]{:S(2)}, u32[]{:S(2)}) collective-permute-start(f32[4,2,2,16]{0,3,2,1:T(8,128)S(1)} %pad_maximum_fusion.34), channel_id=1, source_target_pairs={{0,1},{1,0},{2,3},{3,2},{4,5},{5,4},{6,7},{7,6},{8,9},{9,8},{10,11... | collective-permute-start | bytes 3080 | tf_op jit(solution)/shard_map/ppermute | solution.py:15
  84.1 4.0 %collective-permute-start.3 = (f32[8,2,2,16]{0,3,2,1:T(8,128)S(1)}, f32[8,2,2,16]{0,3,2,1:T(8,128)S(1)}, u32[]{:S(2)}, u32[]{:S(2)}) collective-permute-start(f32[8,2,2,16]{0,3,2,1:T(8,128)S(1)} %maximum_select_fusion), channel_id=1, source_target_pairs={{0,2},{1,3},{2,0},{3,1},{4,6},{5,7},{6,4},{7,5},{8,10},{9,11},{10,... | collective-permute-start | bytes 6152 | tf_op jit(solution)/shard_map/ppermute | solution.py:15
  88.2 4.0 %collective-permute-start.4 = (f32[16,2,2,16]{0,3,2,1:T(8,128)S(1)}, f32[16,2,2,16]{0,3,2,1:T(8,128)S(1)}, u32[]{:S(2)}, u32[]{:S(2)}) collective-permute-start(f32[16,2,2,16]{0,3,2,1:T(8,128)S(1)} %maximum_select_fusion.1), channel_id=1, source_target_pairs={{0,4},{1,5},{2,6},{3,7},{4,0},{5,1},{6,2},{7,3},{8,12},{9,13},{10,... | collective-permute-start | bytes 12296 | tf_op jit(solution)/shard_map/ppermute | solution.py:15
  88.3 9.0 %copy-start.15 = (f32[64]{0:T(128)S(1)}, f32[64]{0:T(128)}, u32[]{:S(2)}) copy-start(f32[64]{0:T(128)} %fusion.84) | copy-start | bytes 772
  88.3 9.6 %copy-start.13 = (f32[2]{0:T(128)S(1)}, f32[2]{0:T(128)}, u32[]{:S(2)}) copy-start(f32[2]{0:T(128)} %constant.64.clone) | copy-start | bytes 28
  88.3 9.7 %copy-start.3 = (f32[2,2,8,16,256]{4,3,2,1,0:T(8,128)S(1)}, f32[2,2,8,16,256]{4,3,2,1,0:T(8,128)}, u32[]{:S(2)}) copy-start(f32[2,2,8,16,256]{4,3,2,1,0:T(8,128)} %param.10) | copy-start | bytes 1572868
  92.3 4.9 %collective-permute-start.5 = (f32[32,2,2,16]{0,3,2,1:T(8,128)S(1)}, f32[32,2,2,16]{0,3,2,1:T(8,128)S(1)}, u32[]{:S(2)}, u32[]{:S(2)}) collective-permute-start(f32[32,2,2,16]{0,3,2,1:T(8,128)S(1)} %maximum_select_fusion.2), channel_id=1, source_target_pairs={{0,8},{1,9},{2,10},{3,11},{4,12},{5,13},{6,14},{7,15},{8,0},{9,1},... | collective-permute-start | bytes 24584 | tf_op jit(solution)/shard_map/ppermute | solution.py:15
  99.5 6.8 %collective-permute-start.6 = (f32[3,2,1,16,256]{4,3,2,1,0:T(8,128)S(1)}, f32[3,2,1,16,256]{4,3,2,1,0:T(8,128)S(1)}, u32[]{:S(2)}, u32[]{:S(2)}) collective-permute-start(f32[3,2,1,16,256]{4,3,2,1,0:T(8,128)S(1)} %get-tuple-element.25), channel_id=1, source_target_pairs={{0,1},{1,2},{2,3},{3,4},{4,5},{5,6},{6,7},{7,8},{8,9},{9,10},{10,1... | collective-permute-start | bytes 294920 | tf_op jit(solution)/shard_map/ppermute | solution.py:29
  99.6 6.7 %collective-permute-start.7 = (f32[3,2,1,16,256]{4,3,2,1,0:T(8,128)S(1)}, f32[3,2,1,16,256]{4,3,2,1,0:T(8,128)S(1)}, u32[]{:S(2)}, u32[]{:S(2)}) collective-permute-start(f32[3,2,1,16,256]{4,3,2,1,0:T(8,128)S(1)} %get-tuple-element.26), channel_id=1, source_target_pairs={{1,0},{2,1},{3,2},{4,3},{5,4},{6,5},{7,6},{8,7},{9,8},{10,9},{11,1... | collective-permute-start | bytes 294920 | tf_op jit(solution)/shard_map/ppermute | solution.py:32
  107.0 63.3 %slice-start = ((f32[15,4,2,2,16]{4,3,2,1,0:T(2,128)}), f32[14,4,2,2,16]{4,3,2,1,0:T(2,128)S(1)}, s32[]{:S(2)}) async-start(f32[15,4,2,2,16]{4,3,2,1,0:T(2,128)} %param.16), calls=%async_computation | async-start | bytes 229376 | tf_op jit(solution)/shard_map/slice | solution.py:136
  107.0 63.3 %copy-start.5 = (f32[16,4,2]{2,1,0:T(4,128)S(1)}, f32[16,4,2]{2,1,0:T(4,128)}, u32[]{:S(2)}) copy-start(f32[16,4,2]{2,1,0:T(4,128)} %copy-done.4) | copy-start | bytes 1540
  170.8 1.4 collective-permute-start.8
  171.7 0.8 copy-start.6
  171.7 0.9 copy-start.7
  171.7 0.9 copy-start.8
  171.7 0.9 copy-start.9
  172.2 11.0 %slice-start.1 = ((f32[15,4,2,2,16]{4,3,2,1,0:T(2,128)}), f32[13,4,2,2,16]{4,3,2,1,0:T(2,128)S(1)}, s32[]{:S(2)}) async-start(f32[15,4,2,2,16]{4,3,2,1,0:T(2,128)} %param.16), calls=%async_computation.1 | async-start | bytes 212992 | tf_op jit(solution)/shard_map/slice | solution.py:136
  172.3 15.8 %copy-start.16 = (f32[64]{0:T(128)S(1)}, f32[64]{0:T(128)}, u32[]{:S(2)}) copy-start(f32[64]{0:T(128)} %fusion.84) | copy-start | bytes 772
  172.3 6.6 %collective-permute-start.9 = (f32[8,2,2,16]{0,3,2,1:T(8,128)S(1)}, f32[8,2,2,16]{0,3,2,1:T(8,128)S(1)}, u32[]{:S(2)}, u32[]{:S(2)}) collective-permute-start(f32[8,2,2,16]{0,3,2,1:T(8,128)S(1)} %maximum_select_fusion.4), channel_id=1, source_target_pairs={{0,2},{1,3},{2,0},{3,1},{4,6},{5,7},{6,4},{7,5},{8,10},{9,11},{10,... | collective-permute-start | bytes 6152 | tf_op jit(solution)/shard_map/ppermute | solution.py:15
  172.6 16.2 %copy-start.1 = (f32[2,2,8,16,256]{4,3,2,1,0:T(8,128)S(1)}, f32[2,2,8,16,256]{4,3,2,1,0:T(8,128)}, u32[]{:S(2)}) copy-start(f32[2,2,8,16,256]{4,3,2,1,0:T(8,128)} %get-tuple-element.24) | copy-start | bytes 1572868
  179.1 4.0 %collective-permute-start.10 = (f32[16,2,2,16]{0,3,2,1:T(8,128)S(1)}, f32[16,2,2,16]{0,3,2,1:T(8,128)S(1)}, u32[]{:S(2)}, u32[]{:S(2)}) collective-permute-start(f32[16,2,2,16]{0,3,2,1:T(8,128)S(1)} %maximum_select_fusion.5), channel_id=1, source_target_pairs={{0,4},{1,5},{2,6},{3,7},{4,0},{5,1},{6,2},{7,3},{8,12},{9,13},{10,... | collective-permute-start | bytes 12296 | tf_op jit(solution)/shard_map/ppermute | solution.py:15
  183.1 4.9 %collective-permute-start.11 = (f32[32,2,2,16]{0,3,2,1:T(8,128)S(1)}, f32[32,2,2,16]{0,3,2,1:T(8,128)S(1)}, u32[]{:S(2)}, u32[]{:S(2)}) collective-permute-start(f32[32,2,2,16]{0,3,2,1:T(8,128)S(1)} %maximum_select_fusion.6), channel_id=1, source_target_pairs={{0,8},{1,9},{2,10},{3,11},{4,12},{5,13},{6,14},{7,15},{8,0},{9,1},... | collective-permute-start | bytes 24584 | tf_op jit(solution)/shard_map/ppermute | solution.py:15
